TPU v7x, 512 devices: a whole 4x8x8 slice. The times are simulated.
512 devices in a mesh: dp: 16 (over z, core), mp: 32 (over y, x).
Axes of the slice: x: 4, y: 8, z: 8, core: 2. Of those that a mesh axis runs over, the one named last changes fastest.
Arguments:
- inputs: bfloat16 [32768, 4096], P('dp', 'mp'), may hold values from -6 to 6
- out_grad: bfloat16 [32768, 4096], P('dp', 'mp'), may hold values from -6 to 6
- mean_state: float32 [6, 64, 64, 64], P(None, 'mp', 'dp'), may hold values from -0.75 to 0.75
- hess_state: float32 [6, 64, 64, 64], P(None, 'mp', 'dp'), may hold values from 2 to 20
- grad_state: float32 [6, 64, 64, 64], P(None, 'mp', 'dp'), may hold values from -1.8 to 1.8
- noise_draw: float32 [16, 6, 64, 64, 64], P('dp', None, 'mp'), may hold values from -6 to 6
Outputs:
- new_mean: float32 [6, 64, 64, 64], P(None, 'mp', 'dp')
- new_hess: float32 [6, 64, 64, 64], P(None, 'mp', 'dp')
- new_grad: float32 [6, 64, 64, 64], P(None, 'mp', 'dp')
All inputs are finite; a program needn't handle non-finite values.
Results may differ from a plain program's by a relative error of at most 0.0018.
Values may be sent and summed in bfloat16 or wider, within the bound.
No kernel may reach another device: no remote copies, remote signals or barrier semaphores. Data moves between devices by JAX's collectives and lax.ppermute only.
A program may use at most 64 MiB of HBM per device.

v0:
```python
import jax
import jax.numpy as jnp
from jax import lax
from jax.sharding import PartitionSpec as P

LAMBDA_SIZE = 100.0
DELTA_DAMP = 0.001
BETA_GRAD = 0.9
BETA_HESS = 0.9
STEP_RATE = 1.0
REDUCE_MODE = "a2a"


def bdot(form, left, right):
    return jnp.einsum(form, left, right, preferred_element_type=jnp.float32)


def silu_slope(value):
    sigm = jax.nn.sigmoid(value)
    return sigm * (1.0 + value * (1.0 - sigm))


def gather_rows(stacked, groups):
    moved = jnp.moveaxis(stacked, 3, 0)
    full = lax.all_gather(moved, "dp", axis=0, tiled=True)
    return jnp.moveaxis(full, 0, 3)


def scatter_rows(stacked, groups):
    s, f, b, r, w = stacked.shape
    split = stacked.reshape(s, f, b, groups, r // groups, w)
    split = jnp.moveaxis(split, 3, 0)
    if REDUCE_MODE == "a2a":
        got = lax.all_to_all(split, "dp", split_axis=0, concat_axis=0, tiled=True)
        summed = jnp.sum(got, axis=0)
    else:
        summed = lax.psum_scatter(split, "dp", scatter_dimension=0, tiled=False)
    return summed


def per_device(inputs, out_grad, mean_state, hess_state, grad_state, noise_draw):
    tokens = inputs.shape[0]
    local_blocks = mean_state.shape[1]
    width = mean_state.shape[3]
    groups = lax.axis_size("dp")
    scale = tokens ** (-0.5)
    full = gather_rows(jnp.stack([mean_state, hess_state]), groups)
    full_mean, full_hess = (full[0], full[1])
    spread = jnp.sqrt(LAMBDA_SIZE * (full_hess + DELTA_DAMP))
    noise = noise_draw[0]
    sampled = (full_mean + noise / spread).astype(jnp.bfloat16)
    in_rows = inputs.reshape(tokens, local_blocks, width)
    grad_rows = out_grad.reshape(tokens, local_blocks, width)
    y_left = bdot("tbr,brc->tcb", in_rows, sampled[0]).astype(jnp.bfloat16)
    y_right = bdot("tbr,brc->tcb", in_rows, sampled[2]).astype(jnp.bfloat16)
    back_outer = bdot("tjc,jic->tij", grad_rows, sampled[5]).astype(jnp.bfloat16)
    first = lax.all_to_all(
        jnp.stack([y_left, y_right, back_outer], axis=1),
        "mp",
        split_axis=2,
        concat_axis=3,
        tiled=True,
    )
    perm_left, perm_right, back_hidden = (first[:, 0], first[:, 1], first[:, 2])
    u_left = bdot("tji,jic->tjc", perm_left, sampled[1])
    u_right = bdot("tji,jic->tjc", perm_right, sampled[3])
    hidden = (jax.nn.silu(u_left) * u_right).astype(jnp.bfloat16)
    outer = bdot("tbr,brc->tcb", hidden, sampled[4]).astype(jnp.bfloat16)
    grad_four = bdot("tbr,tbc->brc", hidden, back_hidden) * scale
    d_hidden = bdot("tbc,brc->tbr", back_hidden, sampled[4])
    gate_grad = (d_hidden * u_right * silu_slope(u_left)).astype(jnp.bfloat16)
    value_grad = (d_hidden * jax.nn.silu(u_left)).astype(jnp.bfloat16)
    grad_one = bdot("tji,tjc->jic", perm_left, gate_grad) * scale
    grad_three = bdot("tji,tjc->jic", perm_right, value_grad) * scale
    back_left = bdot("tjc,jic->tij", gate_grad, sampled[1]).astype(jnp.bfloat16)
    back_right = bdot("tjc,jic->tij", value_grad, sampled[3]).astype(jnp.bfloat16)
    second = lax.all_to_all(
        jnp.stack([outer, back_left, back_right], axis=1),
        "mp",
        split_axis=2,
        concat_axis=3,
        tiled=True,
    )
    mixed_rows, rows_left, rows_right = (second[:, 0], second[:, 1], second[:, 2])
    grad_five = bdot("tji,tjc->jic", mixed_rows, grad_rows) * scale
    grad_zero = bdot("tbr,tbc->brc", in_rows, rows_left) * scale
    grad_two = bdot("tbr,tbc->brc", in_rows, rows_right) * scale
    all_grads = jnp.stack([grad_zero, grad_one, grad_two, grad_three, grad_four, grad_five])
    sums = scatter_rows(jnp.stack([all_grads, all_grads * noise * spread]), groups)
    grad_avg = sums[0] / groups
    hess_avg = sums[1] / groups
    new_grad = BETA_GRAD * grad_state + (1.0 - BETA_GRAD) * grad_avg
    new_hess = (
        BETA_HESS * hess_state
        + (1.0 - BETA_HESS) * hess_avg
        + 0.5 * (1.0 - BETA_HESS) ** 2 * (hess_state - hess_avg) ** 2 / (hess_state + DELTA_DAMP)
    )
    new_mean = mean_state - STEP_RATE * (new_grad + DELTA_DAMP * mean_state) / (
        new_hess + DELTA_DAMP
    )
    return (new_mean, new_hess, new_grad)


def solution(mesh):
    return jax.shard_map(
        per_device,
        mesh=mesh,
        in_specs=(
            P("dp", "mp"),
            P("dp", "mp"),
            P(None, "mp", "dp", None),
            P(None, "mp", "dp", None),
            P(None, "mp", "dp", None),
            P("dp", None, "mp", None, None),
        ),
        out_specs=(P(None, "mp", "dp", None), P(None, "mp", "dp", None), P(None, "mp", "dp", None)),
        check_vma=False,
    )
```

profile of v0, /device:TPU:1, one launch (start us, length us, event | category | flops | bytes accessed | tf_op | source)
XLA Modules:
  0.0 176.5 jit_solution(16778097129029193267)
XLA Ops:
  0.6 0.8 pad_maximum_fusion.2
  1.5 26.8 %all_gather.3 = f32[64,2,6,2,64]{4,3,2,1,0:T(2,128)S(1)} all-gather(f32[4,2,6,2,64]{4,3,2,1,0:T(2,128)S(1)} %bitcast.183), channel_id=1, replica_groups=mesh['dp'=16,'mp'=32] {'dp'}, dimensions={0}, use_global_device_ids=true | all-gather | bytes 417792 | tf_op jit(solution)/shard_map/all_gather | solution.py:25
  29.8 1.2 copy.64
  31.9 1.6 copy.66
  33.5 48.9 %all_to_all.41 = bf16[2048,3,64,2]{0,3,1,2:T(2,128)(2,1)S(1)} all-to-all(bf16[2048,3,64,2]{0,3,1,2:T(2,128)(2,1)S(1)} %copy.66), channel_id=1, replica_groups=mesh['dp'=16,'mp'=32] {'mp'}, dimensions={2} | all-to-all | bytes 3145728 | tf_op jit(solution)/shard_map/all_to_all | solution.py:57
  82.4 1.3 copy.102
  83.6 2.0 %all_to_all.32 = bf16[2048,3,2,64]{0,3,2,1:T(8,128)(2,1)} reshape(bf16[2048,3,2,32,2]{0,4,3,2,1:T(2,128)(2,1)S(1)} %bitcast.163) | data formatting | bytes 3145728 | tf_op jit(solution)/shard_map/all_to_all | solution.py:57
  85.7 1.5 convolution_bitcast_fusion
  89.7 1.6 copy.71
  91.3 42.3 %all_to_all.42 = bf16[2048,3,64,2]{0,3,1,2:T(2,128)(2,1)S(1)} all-to-all(bf16[2048,3,64,2]{0,3,1,2:T(2,128)(2,1)S(1)} %copy.71), channel_id=1, replica_groups=mesh['dp'=16,'mp'=32] {'mp'}, dimensions={2} | all-to-all | bytes 3145728 | tf_op jit(solution)/shard_map/all_to_all | solution.py:77
  133.6 1.3 copy.101
  134.9 2.0 %all_to_all.36 = bf16[2048,3,2,64]{0,3,2,1:T(8,128)(2,1)} reshape(bf16[2048,3,2,32,2]{0,4,3,2,1:T(2,128)(2,1)S(1)} %bitcast.165) | data formatting | bytes 3145728 | tf_op jit(solution)/shard_map/all_to_all | solution.py:77
  136.9 1.4 convolution_multiply_fusion.5
  138.4 1.3 convolution_multiply_fusion.3
  140.4 2.0 %bitcast_dynamic-update-slice_fusion.3 = (f32[1,6,2,64,64]{3,4,2,1,0:T(8,128)}, f32[2,64,64]{1,2,0:T(8,128)S(1)}) fusion(f32[1,6,2,64,64]{3,4,2,1,0:T(8,128)} %constant_dynamic-update-slice_fusion.7, bf16[2048,2,64]{0,2,1:T(8,128)(2,1)} %copy-done.8, bf16[2048,3,2,64]{0,3,2,1:T(8,128)(2,1)S(1)} %copy-done.1), kind=kOutput, calls=%fused_computation.45 | convolution fusion | flops 33562624 | bytes 1146880 | tf_op jit(solution)/shard_map/tji,tjc->jic/dot_general | solution.py:15
  143.2 0.6 constant_dynamic-update-slice_fusion.6
  143.8 1.9 %bitcast_dynamic-update-slice_fusion.2 = (f32[1,6,2,64,64]{3,4,2,1,0:T(8,128)}, f32[2,64,64]{1,2,0:T(8,128)S(1)}) fusion(f32[1,6,2,64,64]{3,4,2,1,0:T(8,128)} %constant_dynamic-update-slice_fusion.6, bf16[2048,2,64]{0,2,1:T(8,128)(2,1)} %copy-done.7, bf16[2048,3,2,64]{0,3,2,1:T(8,128)(2,1)S(1)} %copy-done.1), kind=kOutput, calls=%fused_computation.44 | convolution fusion | flops 33562624 | bytes 1146880 | tf_op jit(solution)/shard_map/tji,tjc->jic/dot_general | solution.py:15
  145.8 1.9 %bitcast_dynamic-update-slice_fusion.1 = (f32[1,6,2,64,64]{3,4,2,1,0:T(8,128)}, f32[2,64,64]{1,2,0:T(8,128)S(1)}) fusion(f32[1,6,2,64,64]{3,4,2,1,0:T(8,128)} %get-tuple-element.11, bf16[2048,2,64]{0,2,1:T(8,128)(2,1)} %copy-done.6, bf16[2048,3,2,64]{0,3,2,1:T(8,128)(2,1)S(1)} %copy-done.1), kind=kOutput, calls=%fused_computation.43 | convolution fusion | flops 33562624 | bytes 1146880 | tf_op jit(solution)/shard_map/tbr,tbc->brc/dot_general | solution.py:15
  147.9 2.0 %bitcast_dynamic-update-slice_fusion = (f32[1,6,2,64,64]{3,4,2,1,0:T(8,128)}, f32[2,64,64]{1,2,0:T(8,128)S(1)}) fusion(f32[1,6,2,64,64]{3,4,2,1,0:T(8,128)} %get-tuple-element.13, bf16[2048,2,64]{0,2,1:T(8,128)(2,1)S(1)} %bitcast.173, bf16[2048,3,2,64]{0,3,2,1:T(8,128)(2,1)} %all_to_all.36), kind=kOutput, calls=%fused_computation.42 | convolution fusion | flops 33562624 | bytes 1146880 | tf_op jit(solution)/shard_map/tji,tjc->jic/dot_general | solution.py:15
  150.0 1.1 sqrt_multiply_fusion
  151.8 0.7 reshape.68
  152.6 20.5 %all_to_all.43 = f32[16,1,6144]{2,1,0:T(1,128)S(1)} all-to-all(f32[16,1,6144]{2,1,0:T(1,128)S(1)} %reshape.68), channel_id=1, replica_groups=mesh['dp'=16,'mp'=32] {'dp'}, dimensions={0} | all-to-all | bytes 786432 | tf_op jit(solution)/shard_map/all_to_all | solution.py:34
  173.6 1.6 reduce
  175.9 0.7 divide_subtract_fusion
  (60 shorter events, 8.3 us)
Async XLA Ops:
  0.6 28.1 %copy-start.9 = (f32[1,6,2,64,64]{4,3,2,1,0:T(8,128)S(1)}, f32[1,6,2,64,64]{4,3,2,1,0:T(8,128)}, u32[]{:S(2)}) copy-start(f32[1,6,2,64,64]{4,3,2,1,0:T(8,128)} %param.11) | copy-start | bytes 589828
  1.5 27.4 %copy-start.5 = (bf16[2048,128]{1,0:T(8,128)(2,1)S(1)}, bf16[2048,128]{1,0:T(8,128)(2,1)}, u32[]{:S(2)}) copy-start(bf16[2048,128]{1,0:T(8,128)(2,1)} %param.6) | copy-start | bytes 1572868
  31.1 0.8 copy-start.2
  85.7 1.6 copy-start
  88.1 0.8 copy-start.8
  88.2 1.0 copy-start.7
  88.2 1.3 copy-start.6
  136.9 3.5 %copy-start.1 = (bf16[2048,3,2,64]{0,3,2,1:T(8,128)(2,1)S(1)}, bf16[2048,3,2,64]{0,3,2,1:T(8,128)(2,1)}, u32[]{:S(2)}) copy-start(bf16[2048,3,2,64]{0,3,2,1:T(8,128)(2,1)} %all_to_all.32) | copy-start | bytes 4718596
  142.5 5.4 %copy-start.3 = (bf16[2048,128]{0,1:T(8,128)(2,1)S(1)}, bf16[2048,128]{0,1:T(8,128)(2,1)}, u32[]{:S(2)}) copy-start(bf16[2048,128]{0,1:T(8,128)(2,1)} %copy-done.2) | copy-start | bytes 1572868
  147.9 3.4 %copy-start.4 = (f32[1,6,2,16,4,64]{5,4,3,2,1,0:T(4,128)S(1)}, f32[1,6,2,16,4,64]{5,4,3,2,1,0:T(4,128)}, u32[]{:S(2)}) copy-start(f32[1,6,2,16,4,64]{5,4,3,2,1,0:T(4,128)} %constant_dynamic-update-slice_fusion.5) | copy-start | bytes 589828
  173.0 2.8 %copy-start.10 = (f32[6,2,4,64]{3,2,1,0:T(4,128)S(1)}, f32[6,2,4,64]{3,2,1,0:T(4,128)}, u32[]{:S(2)}) copy-start(f32[6,2,4,64]{3,2,1,0:T(4,128)} %param.8) | copy-start | bytes 36868
  173.0 2.8 %copy-start.11 = (f32[6,2,4,64]{3,2,1,0:T(4,128)S(1)}, f32[6,2,4,64]{3,2,1,0:T(4,128)}, u32[]{:S(2)}) copy-start(f32[6,2,4,64]{3,2,1,0:T(4,128)} %param.9) | copy-start | bytes 36868
  173.0 2.8 %copy-start.12 = (f32[6,2,4,64]{3,2,1,0:T(4,128)S(1)}, f32[6,2,4,64]{3,2,1,0:T(4,128)}, u32[]{:S(2)}) copy-start(f32[6,2,4,64]{3,2,1,0:T(4,128)} %param.10) | copy-start | bytes 36868
where the time goes:
time: 177 us
  blocking collectives  138 us (78%)
  local copies, waits for them, and re-layouts  17.1 us (10%)
  matrix products  14.9 us (8%)
  other arithmetic  5.01 us (3%)
    all_to_all x1, blocking collectives, per_device(): lax.all_to_all(jnp.stack([y_left, y_right, back_outer], axis=1), 'mp', sp...  48.9 us
    all_to_all x1, blocking collectives, per_device(): lax.all_to_all(jnp.stack([outer, back_left, back_right], axis=1), 'mp', s...  42.3 us
    all_gather x1, blocking collectives, gather_rows(): full = lax.all_gather(moved, 'dp', axis=0, tiled=True)  26.8 us
    all_to_all x1, blocking collectives, scatter_rows(): got = lax.all_to_all(split, 'dp', split_axis=0, concat_axis=0, tiled=True)  20.5 us
    dot_general x15, matrix products, bdot(): return jnp.einsum(form, left, right, preferred_element_type=jnp.float32)  14.9 us
    unnamed x38, local copies, waits for them, and re-layouts  5.49 us

commit v1 on v0

--- a/solution.py
+++ b/solution.py
@@ -74,12 +74,18 @@
     grad_three = bdot("tji,tjc->jic", perm_right, value_grad) * scale
     back_left = bdot("tjc,jic->tij", gate_grad, sampled[1]).astype(jnp.bfloat16)
     back_right = bdot("tjc,jic->tij", value_grad, sampled[3]).astype(jnp.bfloat16)
-    second = lax.all_to_all(
-        jnp.stack([outer, back_left, back_right], axis=1),
-        "mp",
-        split_axis=2,
-        concat_axis=3,
-        tiled=True,
+    second = jnp.concatenate(
+        lax.all_to_all(
+            jnp.stack(
+                jnp.split(
+                    jnp.stack([outer, back_left, back_right], axis=1), lax.axis_size("mp"), axis=2
+                )
+            ),
+            "mp",
+            0,
+            0,
+        ),
+        axis=3,
     )
     mixed_rows, rows_left, rows_right = (second[:, 0], second[:, 1], second[:, 2])
     grad_five = bdot("tji,tjc->jic", mixed_rows, grad_rows) * scale

time: 177 us -> 178 us (level)
    all_to_all x2 -> x0, local copies, waits for them, and re-layouts: 3.3 us -> none  [per_device(): lax.all_to_all(jnp.stack([outer, back_left, back_right], axis=1), 'mp', s...]
    slice x0 -> x1, local copies, waits for them, and re-layouts: none -> 2.3 us  [per_device(): second[:, 0]]
    unnamed x38 -> x67, local copies, waits for them, and re-layouts: 5.49 us -> 7.42 us
    reshape x0 -> x1, local copies, waits for them, and re-layouts: none -> 1.79 us  [per_device(): jnp.concatenate(lax.all_to_all(jnp.stack(jnp.split(jnp.stack([outer, back...]
where the time goes in v1:
time: 178 us; the launch traced here: 177 us
  blocking collectives  138 us (78%)
  local copies, waits for them, and re-layouts  18.3 us (10%)
  matrix products  14.1 us (8%)
  other arithmetic  5.04 us (3%)
    all_to_all x1, blocking collectives, per_device(): lax.all_to_all(jnp.stack([y_left, y_right, back_outer], axis=1), 'mp', sp...  48.9 us
    all_to_all x1, blocking collectives, per_device(): lax.all_to_all(jnp.stack(jnp.split(jnp.stack([outer, back_left, back_righ...  42.3 us
    all_gather x1, blocking collectives, gather_rows(): full = lax.all_gather(moved, 'dp', axis=0, tiled=True)  26.8 us
    all_to_all x1, blocking collectives, scatter_rows(): got = lax.all_to_all(split, 'dp', split_axis=0, concat_axis=0, tiled=True)  20.5 us
    dot_general x15, matrix products, bdot(): return jnp.einsum(form, left, right, preferred_element_type=jnp.float32)  14.1 us
    unnamed x67, local copies, waits for them, and re-layouts  7.42 us

profile of v1, /device:TPU:1, one launch (start us, length us, event | category | flops | bytes accessed | tf_op | source)
XLA Modules:
  0.0 177.0 jit_solution(2309477394520920967)
XLA Ops:
  0.6 0.8 pad_maximum_fusion.2
  1.5 26.8 %all_gather.3 = f32[64,2,6,2,64]{4,3,2,1,0:T(2,128)S(1)} all-gather(f32[4,2,6,2,64]{4,3,2,1,0:T(2,128)S(1)} %bitcast.307), channel_id=1, replica_groups=mesh['dp'=16,'mp'=32] {'dp'}, dimensions={0}, use_global_device_ids=true | all-gather | bytes 417792 | tf_op jit(solution)/shard_map/all_gather | solution.py:25
  29.8 1.2 copy.66
  31.9 1.6 copy.68
  33.5 48.9 %all_to_all.28 = bf16[2048,3,64,2]{0,3,1,2:T(2,128)(2,1)S(1)} all-to-all(bf16[2048,3,64,2]{0,3,1,2:T(2,128)(2,1)S(1)} %copy.68), channel_id=1, replica_groups=mesh['dp'=16,'mp'=32] {'mp'}, dimensions={2} | all-to-all | bytes 3145728 | tf_op jit(solution)/shard_map/all_to_all | solution.py:57
  82.4 1.3 copy.115
  83.6 2.0 %all_to_all.22 = bf16[2048,3,2,64]{0,3,2,1:T(8,128)(2,1)} reshape(bf16[2048,3,2,32,2]{0,4,3,2,1:T(2,128)(2,1)S(1)} %bitcast.288) | data formatting | bytes 3145728 | tf_op jit(solution)/shard_map/all_to_all | solution.py:57
  85.7 1.5 convolution_bitcast_fusion
  87.5 0.6 multiply_convert_fusion.2
  91.8 42.3 %all_to_all.29 = bf16[32,2048,3,2,2]{1,3,4,2,0:T(2,128)(2,1)S(1)} all-to-all(bf16[32,2048,3,2,2]{1,3,4,2,0:T(2,128)(2,1)S(1)} %constant_dynamic-update-slice_fusion), channel_id=1, replica_groups=mesh['dp'=16,'mp'=32] {'mp'}, dimensions={0} | all-to-all | bytes 3145728 | tf_op jit(solution)/shard_map/all_to_all | solution.py:78
  134.1 1.8 %copy.73 = bf16[2048,3,2,32,2]{0,2,4,3,1:T(2,128)(2,1)S(1)} copy(bf16[2048,3,2,32,2]{0,2,4,1,3:T(2,128)(2,1)S(1)} %bitcast.289) | data formatting | bytes 3145728 | tf_op jit(solution)/shard_map/reshape | solution.py:77
  135.9 2.3 %fusion.17 = (bf16[2048,1,2,64]{0,2,3,1:T(2,128)(2,1)}, bf16[2048,1,2,64]{0,2,3,1:T(2,128)(2,1)}, bf16[2048,1,2,64]{0,2,3,1:T(2,128)(2,1)S(1)}) fusion(bf16[2048,3,2,64]{0,2,3,1:T(2,128)(2,1)S(1)} %bitcast.286), kind=kLoop, calls=%fused_computation.135 | loop fusion | bytes 3145728 | tf_op jit(solution)/shard_map/slice | solution.py:90
  138.7 0.6 constant_dynamic-update-slice_fusion.43
  139.3 2.0 %constant_dynamic-update-slice_fusion.42 = (f32[1,6,2,64,64]{3,4,2,1,0:T(8,128)}, f32[2,64,64]{1,2,0:T(8,128)S(1)}) fusion(f32[1,6,2,64,64]{3,4,2,1,0:T(8,128)} %constant_dynamic-update-slice_fusion.43, bf16[2048,2,64]{0,2,1:T(8,128)(2,1)} %copy-done.7, bf16[2048,3,2,64]{0,3,2,1:T(8,128)(2,1)S(1)} %copy-done), kind=kOutput, calls=%fused_computation.83 | convolution fusion | flops 33562624 | bytes 1146880 | tf_op jit(solution)/shard_map/tji,tjc->jic/dot_general | solution.py:15
  141.3 0.6 constant_dynamic-update-slice_fusion.37
  142.0 1.4 convolution_multiply_fusion.3
  144.1 1.9 %constant_dynamic-update-slice_fusion.40 = (f32[1,6,2,64,64]{3,4,2,1,0:T(8,128)}, f32[2,64,64]{1,2,0:T(8,128)S(1)}) fusion(f32[1,6,2,64,64]{3,4,2,1,0:T(8,128)} %constant_dynamic-update-slice_fusion.41, bf16[2048,2,64]{0,2,1:T(8,128)(2,1)} %copy-done.6, bf16[2048,3,2,64]{0,3,2,1:T(8,128)(2,1)S(1)} %copy-done), kind=kOutput, calls=%fused_computation.81 | convolution fusion | flops 33562624 | bytes 1146880 | tf_op jit(solution)/shard_map/tji,tjc->jic/dot_general | solution.py:15
  146.1 1.9 %constant_dynamic-update-slice_fusion.39 = (f32[1,6,2,64,64]{3,4,2,1,0:T(8,128)}, f32[2,64,64]{1,2,0:T(8,128)S(1)}) fusion(f32[1,6,2,64,64]{3,4,2,1,0:T(8,128)} %get-tuple-element.14, bf16[2048,2,64]{0,2,1:T(8,128)(2,1)} %copy-done.5, bf16[2048,3,2,64]{0,3,2,1:T(8,128)(2,1)S(1)} %copy-done), kind=kOutput, calls=%fused_computation.80 | convolution fusion | flops 33562624 | bytes 1146880 | tf_op jit(solution)/shard_map/tbr,tbc->brc/dot_general | solution.py:15
  148.2 2.1 %constant_dynamic-update-slice_fusion.38 = (f32[1,6,2,64,64]{3,4,2,1,0:T(8,128)}, f32[2,64,64]{1,2,0:T(8,128)S(1)}) fusion(f32[1,6,2,64,64]{3,4,2,1,0:T(8,128)} %get-tuple-element.16, bf16[2048,2,64]{0,2,1:T(8,128)(2,1)S(1)} %bitcast.297, bf16[2048,1,2,64]{0,2,3,1:T(2,128)(2,1)} %get-tuple-element.9), kind=kOutput, calls=%fused_computation.79 | convolution fusion | flops 33562624 | bytes 1146880 | tf_op jit(solution)/shard_map/tji,tjc->jic/dot_general | solution.py:15
  150.4 1.1 sqrt_multiply_fusion
  152.3 0.7 reshape.76
  153.0 20.5 %all_to_all.30 = f32[16,1,6144]{2,1,0:T(1,128)S(1)} all-to-all(f32[16,1,6144]{2,1,0:T(1,128)S(1)} %reshape.76), channel_id=1, replica_groups=mesh['dp'=16,'mp'=32] {'dp'}, dimensions={0} | all-to-all | bytes 786432 | tf_op jit(solution)/shard_map/all_to_all | solution.py:34
  174.0 1.6 reduce
  176.3 0.7 divide_subtract_fusion
  (89 shorter events, 9.4 us)
Async XLA Ops:
  0.6 28.1 %copy-start.8 = (f32[1,6,2,64,64]{4,3,2,1,0:T(8,128)S(1)}, f32[1,6,2,64,64]{4,3,2,1,0:T(8,128)}, u32[]{:S(2)}) copy-start(f32[1,6,2,64,64]{4,3,2,1,0:T(8,128)} %param.11) | copy-start | bytes 589828
  1.5 27.4 %copy-start.4 = (bf16[2048,128]{1,0:T(8,128)(2,1)S(1)}, bf16[2048,128]{1,0:T(8,128)(2,1)}, u32[]{:S(2)}) copy-start(bf16[2048,128]{1,0:T(8,128)(2,1)} %param.6) | copy-start | bytes 1572868
  31.1 0.8 copy-start.1
  85.7 1.6 copy-start
  88.2 0.8 copy-start.5
  88.2 1.0 copy-start.6
  88.2 1.1 copy-start.7
  143.4 4.8 %copy-start.2 = (bf16[2048,128]{0,1:T(8,128)(2,1)S(1)}, bf16[2048,128]{0,1:T(8,128)(2,1)}, u32[]{:S(2)}) copy-start(bf16[2048,128]{0,1:T(8,128)(2,1)} %copy-done.1) | copy-start | bytes 1572868
  148.2 3.5 %copy-start.3 = (f32[1,6,2,16,4,64]{5,4,3,2,1,0:T(4,128)S(1)}, f32[1,6,2,16,4,64]{5,4,3,2,1,0:T(4,128)}, u32[]{:S(2)}) copy-start(f32[1,6,2,16,4,64]{5,4,3,2,1,0:T(4,128)} %constant_dynamic-update-slice_fusion.37) | copy-start | bytes 589828
  173.5 2.8 %copy-start.9 = (f32[6,2,4,64]{3,2,1,0:T(4,128)S(1)}, f32[6,2,4,64]{3,2,1,0:T(4,128)}, u32[]{:S(2)}) copy-start(f32[6,2,4,64]{3,2,1,0:T(4,128)} %param.8) | copy-start | bytes 36868
  173.5 2.8 %copy-start.10 = (f32[6,2,4,64]{3,2,1,0:T(4,128)S(1)}, f32[6,2,4,64]{3,2,1,0:T(4,128)}, u32[]{:S(2)}) copy-start(f32[6,2,4,64]{3,2,1,0:T(4,128)} %param.9) | copy-start | bytes 36868
  173.5 2.8 %copy-start.11 = (f32[6,2,4,64]{3,2,1,0:T(4,128)S(1)}, f32[6,2,4,64]{3,2,1,0:T(4,128)}, u32[]{:S(2)}) copy-start(f32[6,2,4,64]{3,2,1,0:T(4,128)} %param.10) | copy-start | bytes 36868
